TPU v7x, 128 devices: a whole 4x4x4 slice. The times are simulated.
128 devices in a mesh: param: 16 (over x, y_hi, core), ex: 8 (over y_lo, z).
Axes of the slice: x: 4, y: 4 (y_hi: 2, y_lo: 2; y = y_hi * 2 + y_lo), z: 4, core: 2. Of those that a mesh axis runs over, the one named last changes fastest.
Arguments:
- grads: float32 [98304, 4096], P('param', 'ex'), may hold values from -6 to 6
- projection: bfloat16 [98304, 1024], P('param'), may hold values from -6 to 6
- whitener: float32 [1024, 1024], P('param'), may hold values from -1 to 3
Outputs:
- scores: float32 [4096, 4096], P('ex', 'param')
All inputs are finite; a program needn't handle non-finite values.
Results may differ from a plain program's by a relative error of at most 0.0052.
Values may be sent and summed in bfloat16 or wider, within the bound.
No kernel may reach another device: no remote copies, remote signals or barrier semaphores. Data moves between devices by JAX's collectives and lax.ppermute only.
A program may use at most 128 MiB of HBM per device.

v0:
```python
import math
import jax
import jax.numpy as jnp
from jax import lax
from jax.sharding import PartitionSpec as P


def body(grads, projection, whitener):
    low_grads = grads.astype(jnp.bfloat16)
    partial_value = lax.dot_general(
        projection, low_grads, (((0,), (0,)), ((), ())), preferred_element_type=jnp.float32
    )
    param_count = lax.axis_size("param")
    ex_count = lax.axis_size("ex")
    norm_factor = 1.0 / math.sqrt(grads.shape[0] * param_count)
    whole_whitener = lax.all_gather(whitener, "param", axis=0, tiled=True)
    sketch_rows = partial_value.shape[0]
    local_width = grads.shape[1]
    total_width = local_width * ex_count
    tile_width = total_width // param_count
    col_start = lax.axis_index("param") * tile_width
    sketch = lax.psum(partial_value, "param") * norm_factor
    whitened = jnp.dot(whole_whitener, sketch, precision=lax.Precision.HIGHEST).astype(jnp.bfloat16)
    all_columns = lax.all_gather(whitened, "ex", axis=1, tiled=True)
    row_start = lax.axis_index("ex") * local_width
    row_block = lax.dynamic_slice_in_dim(all_columns, row_start, local_width, 1)
    col_block = lax.dynamic_slice_in_dim(all_columns, col_start, tile_width, 1)
    tile = lax.dot_general(
        row_block, col_block, (((0,), (0,)), ((), ())), preferred_element_type=jnp.float32
    )
    return tile / sketch_rows


def solution(mesh):
    return jax.shard_map(
        body,
        mesh=mesh,
        in_specs=(P("param", "ex"), P("param", None), P("param", None)),
        out_specs=P("ex", "param"),
        check_vma=False,
    )
```

profile of v0, /device:TPU:1, one launch (start us, length us, event | category | flops | bytes accessed | tf_op | source)
XLA Modules:
  0.0 344.9 jit_solution(1237545374964463168)
XLA Ops:
  6.5 0.0 all-reduce.2.cloned.1.call-start
  6.5 14.3 %fusion = f32[1024,512]{1,0:T(8,128)} fusion(bf16[6144,1024]{1,0:T(8,128)(2,1)} %param.4, f32[6144,512]{1,0:T(8,128)} %param.3), kind=kOutput, calls=%fused_computation | convolution fusion | flops 6445596672 | bytes 27262976 | tf_op jit(solution)/shard_map/dot_general | solution.py:10
  20.9 0.0 all-reduce.2.cloned.1.call-update
  20.9 0.0 all-gather.3.cloned.1.call-start
  21.0 0.7 all-gather.3.cloned.1.call-update
  21.7 0.0 all-gather.5.cloned.1.call-start
  21.7 146.6 %all-reduce.2.cloned.1.call-done = f32[1024,512]{1,0:T(8,128)} async-done(((f32[1024,512]{1,0:T(8,128)}), f32[1024,512]{1,0:T(8,128)}) %all-reduce.2.cloned.1.call-update) | async-done | bytes 2097168 | tf_op jit(solution)/shard_map/psum | solution.py:22
  168.3 60.1 %all-gather.3.cloned.1.call-done = f32[1024,1024]{1,0:T(8,128)} async-done(((f32[64,1024]{1,0:T(8,128)}), f32[1024,1024]{1,0:T(8,128)}) %all-gather.3.cloned.1.call-update) | async-done | bytes 4194320 | tf_op jit(solution)/shard_map/all_gather | solution.py:16
  228.4 16.6 %fusion.7 = bf16[1024,512]{0,1:T(8,128)(2,1)} fusion(f32[1024,1024]{1,0:T(8,128)} %all-gather.3.cloned.1.call-done, f32[1024,512]{1,0:T(8,128)} %all-reduce.2.cloned.1.call-done), kind=kOutput, calls=%fused_computation.5 | convolution fusion | flops 6443499520 | bytes 7340032 | tf_op jit(solution)/shard_map/dot_general | solution.py:23
  245.0 0.0 all-gather.5.cloned.1.call-update
  245.0 90.7 %all-gather.5.cloned.1.call-done = bf16[1024,4096]{0,1:T(8,128)(2,1)} async-done(((bf16[1024,512]{0,1:T(8,128)(2,1)}), bf16[1024,4096]{0,1:T(8,128)(2,1)}) %all-gather.5.cloned.1.call-update) | async-done | bytes 8388624 | tf_op jit(solution)/shard_map/all_gather | solution.py:24
  335.7 2.6 convolution_multiply_fusion
Async XLA Ops:
  6.5 161.7 %all-reduce.2.cloned.1.call-start = ((), (), s32[]{:S(2)}) async-start(), calls=%async_computation | async-start | bytes 4194304 | tf_op jit(solution)/shard_map/psum | solution.py:22
  20.9 207.5 %all-gather.3.cloned.1.call-start = ((), (), s32[]{:S(2)}) async-start(), calls=%async_computation.1 | async-start | bytes 4456448 | tf_op jit(solution)/shard_map/all_gather | solution.py:16
  21.7 314.1 %all-gather.5.cloned.1.call-start = ((), (), s32[]{:S(2)}) async-start(), calls=%async_computation.2 | async-start | bytes 9437184 | tf_op jit(solution)/shard_map/all_gather | solution.py:24
Sparse Core Ops, SparseCore 0:
  21.0 147.1 all-reduce.1
  170.7 57.6 all-gather.2
  245.1 90.5 all-gather.4
where the time goes:
time: 345 us
  waiting for transfers between devices  298 us (86%)
  matrix products  33.6 us (10%)
  between operations  13.1 us (4%)
    psum x1, waiting for transfers between devices, body(): sketch = lax.psum(partial_value, 'param') * norm_factor  147 us
    all_gather x1, waiting for transfers between devices, body(): all_columns = lax.all_gather(whitened, 'ex', axis=1, tiled=True)  90.7 us
    all_gather x1, waiting for transfers between devices, body(): whole_whitener = lax.all_gather(whitener, 'param', axis=0, tiled=True)  60.1 us
    dot_general x1, matrix products, body(): jnp.dot(whole_whitener, sketch, precision=lax.Precision.HIGHEST)  16.6 us
    dot_general x1, matrix products, body(): lax.dot_general(projection, low_grads, (((0,), (0,)), ((), ())), preferre...  14.3 us
  transfers between devices with their start and end apart: 3, of which 3 were waited for; matrix products, arithmetic and copies ran while one was open for 0% of the time, Pallas kernels for 0%

commit v1 on v0

--- a/solution.py
+++ b/solution.py
@@ -13,7 +13,12 @@
     param_count = lax.axis_size("param")
     ex_count = lax.axis_size("ex")
     norm_factor = 1.0 / math.sqrt(grads.shape[0] * param_count)
-    whole_whitener = lax.all_gather(whitener, "param", axis=0, tiled=True)
+    whole_whitener = jnp.concatenate(
+        lax.all_to_all(
+            jnp.stack([whitener for _ in range(lax.axis_size("param"))], 0), "param", 0, 0
+        ),
+        0,
+    )
     sketch_rows = partial_value.shape[0]
     local_width = grads.shape[1]
     total_width = local_width * ex_count

time: 345 us -> 318 us (0.922)
  waiting for transfers between devices: 298 us -> 259 us
  starting transfers between devices: 0.08 us -> 8.52 us
  local copies, waits for them, and re-layouts: 0 us -> 3.45 us
    all_gather x1 -> x0, waiting for transfers between devices: 60.1 us -> none  [body(): whole_whitener = lax.all_gather(whitener, 'param', axis=0, tiled=True)]
    psum x1, waiting for transfers between devices: 147 us -> 166 us  [body(): sketch = lax.psum(partial_value, 'param') * norm_factor]
    all_to_all x0 -> x1, starting transfers between devices: none -> 8.45 us  [body(): lax.all_to_all(jnp.stack([whitener for _ in range(lax.axis_size('param'))...]
  transfers between devices with their start and end apart: 3 -> 3, of which waited for: 3 -> 2; matrix products, arithmetic and copies ran while one was open for 0% -> 4% of each run, Pallas kernels for 0% -> 0%
where the time goes in v1:
time: 318 us
  waiting for transfers between devices  259 us (81%)
  matrix products  33.5 us (11%)
  between operations  13.4 us (4%)
  starting transfers between devices  8.52 us (3%)
  local copies, waits for them, and re-layouts  3.45 us (1%)
    psum x1, waiting for transfers between devices, body(): sketch = lax.psum(partial_value, 'param') * norm_factor  166 us
    all_gather x1, waiting for transfers between devices, body(): all_columns = lax.all_gather(whitened, 'ex', axis=1, tiled=True)  93.6 us
    dot_general x1, matrix products, body(): jnp.dot(whole_whitener, sketch, precision=lax.Precision.HIGHEST)  16.6 us
    dot_general x1, matrix products, body(): lax.dot_general(projection, low_grads, (((0,), (0,)), ((), ())), preferre...  14.3 us
    all_to_all x1, starting transfers between devices, body(): lax.all_to_all(jnp.stack([whitener for _ in range(lax.axis_size('param'))...  8.45 us
  transfers between devices with their start and end apart: 3, of which 2 were waited for; matrix products, arithmetic and copies ran while one was open for 4% of the time, Pallas kernels for 0%

profile of v1, /device:TPU:1, one launch (start us, length us, event | category | flops | bytes accessed | tf_op | source)
XLA Modules:
  0.0 318.1 jit_solution(13056351178425769629)
XLA Ops:
  6.5 3.4 %stack.2 = f32[16,64,1024]{2,1,0:T(8,128)} broadcast(f32[64,1024]{1,0:T(8,128)} %param.5), dimensions={1,2} | broadcast | bytes 4456448 | tf_op jit(solution)/shard_map/stack | solution.py:18
  10.0 8.4 %all-to-all-start = ((f32[16,64,1024]{2,1,0:T(8,128)}), f32[16,64,1024]{2,1,0:T(8,128)}, u32[]{:S(2)}, u32[]{:S(2)}) async-start(f32[16,64,1024]{2,1,0:T(8,128)} %stack.2), calls=%async_computation | async-start | bytes 8388608 | tf_op jit(solution)/shard_map/all_to_all | solution.py:17
  18.4 0.0 all-reduce.2.cloned.1.call-start
  18.5 14.3 %fusion = f32[1024,512]{1,0:T(8,128)} fusion(bf16[6144,1024]{1,0:T(8,128)(2,1)} %param.4, f32[6144,512]{1,0:T(8,128)} %param.3), kind=kOutput, calls=%fused_computation | convolution fusion | flops 6445596672 | bytes 27262976 | tf_op jit(solution)/shard_map/dot_general | solution.py:10
  32.8 0.0 all-reduce.2.cloned.1.call-update
  32.8 0.0 all-gather.2.cloned.1.call-start
  32.8 165.6 %all-reduce.2.cloned.1.call-done = f32[1024,512]{1,0:T(8,128)} async-done(((f32[1024,512]{1,0:T(8,128)}), f32[1024,512]{1,0:T(8,128)}) %all-reduce.2.cloned.1.call-update) | async-done | bytes 2097168 | tf_op jit(solution)/shard_map/psum | solution.py:27
  198.4 0.0 all-to-all-done
  198.4 16.6 %fusion.7 = bf16[1024,512]{0,1:T(8,128)(2,1)} fusion(f32[1024,1024]{1,0:T(8,128)} %bitcast, f32[1024,512]{1,0:T(8,128)} %all-reduce.2.cloned.1.call-done), kind=kOutput, calls=%fused_computation.5 | convolution fusion | flops 6443499520 | bytes 7340032 | tf_op jit(solution)/shard_map/dot_general | solution.py:28
  215.0 0.0 all-gather.2.cloned.1.call-update
  215.0 93.6 %all-gather.2.cloned.1.call-done = bf16[1024,4096]{0,1:T(8,128)(2,1)} async-done(((bf16[1024,512]{0,1:T(8,128)(2,1)}), bf16[1024,4096]{0,1:T(8,128)(2,1)}) %all-gather.2.cloned.1.call-update) | async-done | bytes 8388624 | tf_op jit(solution)/shard_map/all_gather | solution.py:29
  308.6 2.6 convolution_multiply_fusion
Async XLA Ops:
  10.0 188.5 %all-to-all-start = ((f32[16,64,1024]{2,1,0:T(8,128)}), f32[16,64,1024]{2,1,0:T(8,128)}, u32[]{:S(2)}, u32[]{:S(2)}) async-start(f32[16,64,1024]{2,1,0:T(8,128)} %stack.2), calls=%async_computation | async-start | bytes 8388608 | tf_op jit(solution)/shard_map/all_to_all | solution.py:17
  18.4 180.0 %all-reduce.2.cloned.1.call-start = ((), (), s32[]{:S(2)}) async-start(), calls=%async_computation.1 | async-start | bytes 4194304 | tf_op jit(solution)/shard_map/psum | solution.py:27
  32.8 275.8 %all-gather.2.cloned.1.call-start = ((), (), s32[]{:S(2)}) async-start(), calls=%async_computation.2 | async-start | bytes 9437184 | tf_op jit(solution)/shard_map/all_gather | solution.py:29
Sparse Core Ops, SparseCore 0:
  32.9 165.4 all-reduce.1
  215.2 93.4 all-gather.1

commit v2 on v0

--- a/solution.py
+++ b/solution.py
@@ -3,6 +3,12 @@
 import jax.numpy as jnp
 from jax import lax
 from jax.sharding import PartitionSpec as P
+
+
+def summed_here(x, axis):
+    terms = lax.all_gather(x, axis, axis=0, tiled=False)
+    total = terms.sum(axis=0)
+    return total
 
 
 def body(grads, projection, whitener):
@@ -19,7 +25,7 @@
     total_width = local_width * ex_count
     tile_width = total_width // param_count
     col_start = lax.axis_index("param") * tile_width
-    sketch = lax.psum(partial_value, "param") * norm_factor
+    sketch = summed_here(partial_value, "param") * norm_factor
     whitened = jnp.dot(whole_whitener, sketch, precision=lax.Precision.HIGHEST).astype(jnp.bfloat16)
     all_columns = lax.all_gather(whitened, "ex", axis=1, tiled=True)
     row_start = lax.axis_index("ex") * local_width

time: 345 us -> 384 us (1.11)
  waiting for transfers between devices: 298 us -> 325 us
  other arithmetic: 0 us -> 12.8 us
    all_gather x0 -> x1, waiting for transfers between devices: none -> 191 us  [summed_here(): terms = lax.all_gather(x, axis, axis=0, tiled=False)]
    psum x1 -> x0, waiting for transfers between devices: 147 us -> none  [body(): sketch = lax.psum(partial_value, 'param') * norm_factor]
    all_gather x1, waiting for transfers between devices: 60.1 us -> 43.1 us  [body(): whole_whitener = lax.all_gather(whitener, 'param', axis=0, tiled=True)]
    reduce_sum x0 -> x1, other arithmetic: none -> 12.8 us  [summed_here(): total = terms.sum(axis=0)]
  transfers between devices with their start and end apart: 3 -> 3, of which waited for: 3 -> 3; matrix products, arithmetic and copies ran while one was open for 0% -> 3% of each run, Pallas kernels for 0% -> 0%
where the time goes in v2:
time: 384 us
  waiting for transfers between devices  325 us (85%)
  matrix products  33 us (9%)
  between operations  13.1 us (3%)
  other arithmetic  12.8 us (3%)
    all_gather x1, waiting for transfers between devices, summed_here(): terms = lax.all_gather(x, axis, axis=0, tiled=False)  191 us
    all_gather x1, waiting for transfers between devices, body(): all_columns = lax.all_gather(whitened, 'ex', axis=1, tiled=True)  90.7 us
    all_gather x1, waiting for transfers between devices, body(): whole_whitener = lax.all_gather(whitener, 'param', axis=0, tiled=True)  43.1 us
    dot_general x1, matrix products, body(): jnp.dot(whole_whitener, sketch, precision=lax.Precision.HIGHEST)  16 us
    dot_general x1, matrix products, body(): lax.dot_general(projection, low_grads, (((0,), (0,)), ((), ())), preferre...  14.4 us
    reduce_sum x1, other arithmetic, summed_here(): total = terms.sum(axis=0)  12.8 us
  transfers between devices with their start and end apart: 3, of which 3 were waited for; matrix products, arithmetic and copies ran while one was open for 3% of the time, Pallas kernels for 0%

profile of v2, /device:TPU:1, one launch (start us, length us, event | category | flops | bytes accessed | tf_op | source)
XLA Modules:
  0.0 384.2 jit_solution(12166970372623265708)
XLA Ops:
  6.5 0.0 all-gather.9.cloned.1.call-start
  6.5 14.4 %fusion = f32[1024,512]{1,0:T(8,128)} fusion(bf16[6144,1024]{1,0:T(8,128)(2,1)} %param.4, f32[6144,512]{1,0:T(8,128)} %param.3), kind=kOutput, calls=%fused_computation | convolution fusion | flops 6445596672 | bytes 27262976 | tf_op jit(solution)/shard_map/dot_general | solution.py:16
  21.0 0.0 all-gather.9.cloned.1.call-update
  21.0 0.0 all-gather.5.cloned.1.call-start
  21.0 0.7 all-gather.5.cloned.1.call-update
  21.7 0.0 all-gather.7.cloned.1.call-start
  21.8 190.6 %all-gather.9.cloned.1.call-done = f32[16384,512]{1,0:T(8,128)} async-done(((f32[1024,512]{1,0:T(8,128)}), f32[16384,512]{1,0:T(8,128)}) %all-gather.9.cloned.1.call-update) | async-done | bytes 33554448 | tf_op jit(solution)/shard_map/all_gather | solution.py:9
  212.4 12.8 %reduce_sum.9 = f32[1024,512]{1,0:T(8,128)S(1)} reduce(f32[16,1024,512]{2,1,0:T(8,128)} %bitcast.5, f32[]{:T(128)} %constant.4.clone.1), dimensions={0}, to_apply=%region_0.0 | reduce | flops 7864320 | bytes 35651588 | tf_op jit(solution)/shard_map/reduce_sum | solution.py:10
  225.2 43.1 %all-gather.5.cloned.1.call-done = f32[1024,1024]{1,0:T(8,128)} async-done(((f32[64,1024]{1,0:T(8,128)}), f32[1024,1024]{1,0:T(8,128)}) %all-gather.5.cloned.1.call-update) | async-done | bytes 4194320 | tf_op jit(solution)/shard_map/all_gather | solution.py:22
  268.4 16.0 %fusion.7 = bf16[1024,512]{0,1:T(8,128)(2,1)} fusion(f32[1024,1024]{1,0:T(8,128)} %all-gather.5.cloned.1.call-done, f32[1024,512]{1,0:T(8,128)S(1)} %reduce_sum.9), kind=kOutput, calls=%fused_computation.5 | convolution fusion | flops 6443499520 | bytes 7340032 | tf_op jit(solution)/shard_map/dot_general | solution.py:29
  284.3 0.0 all-gather.7.cloned.1.call-update
  284.4 90.7 %all-gather.7.cloned.1.call-done = bf16[1024,4096]{0,1:T(8,128)(2,1)} async-done(((bf16[1024,512]{0,1:T(8,128)(2,1)}), bf16[1024,4096]{0,1:T(8,128)(2,1)}) %all-gather.7.cloned.1.call-update) | async-done | bytes 8388624 | tf_op jit(solution)/shard_map/all_gather | solution.py:30
  375.1 2.6 convolution_multiply_fusion
Async XLA Ops:
  6.5 205.9 %all-gather.9.cloned.1.call-start = ((), (), s32[]{:S(2)}) async-start(), calls=%async_computation.2 | async-start | bytes 35651584 | tf_op jit(solution)/shard_map/all_gather | solution.py:9
  21.0 247.4 %all-gather.5.cloned.1.call-start = ((), (), s32[]{:S(2)}) async-start(), calls=%async_computation | async-start | bytes 4456448 | tf_op jit(solution)/shard_map/all_gather | solution.py:22
  21.7 353.3 %all-gather.7.cloned.1.call-start = ((), (), s32[]{:S(2)}) async-start(), calls=%async_computation.1 | async-start | bytes 9437184 | tf_op jit(solution)/shard_map/all_gather | solution.py:30
Sparse Core Ops, SparseCore 0:
  21.1 191.2 all-gather.8
  214.8 53.5 all-gather.4
  284.5 90.5 all-gather.6
